TPU v7x, 32 devices: a whole 2x2x4 slice. The times are simulated.
32 devices in a mesh: span: 8 (over z, x), slab: 4 (over y, core).
Axes of the slice: x: 2, y: 2, z: 4, core: 2. Of those that a mesh axis runs over, the one named last changes fastest.
Arguments:
- features: float32 [512, 32, 2048], P('slab', None, 'span'), may hold values from -6 to 6
- spectral_weight: float32 [512, 2048], P('span', 'slab'), may hold values from -2.5 to 2.5
- local_weight: float32 [32, 32], replicated, may hold values from -1 to 1
- bias_vector: float32 [32], replicated, may hold values from -1 to 1
Outputs:
- activated: float32 [512, 32, 2048], P('slab', None, 'span')
All inputs are finite; a program needn't handle non-finite values.
Results may differ from a plain program's by a relative error of at most 0.00005.
Values sent between devices are 32-bit elements; how exact they have to be, the bound alone decides.
No kernel may reach another device: no remote copies, remote signals or barrier semaphores. Data moves between devices by JAX's collectives and lax.ppermute only.
A program may use at most 128 MiB of HBM per device.

v0:
```python
import math
import jax
import jax.numpy as jnp
from jax import lax
from jax.sharding import PartitionSpec as P


def tables(number, length, span_total):
    wavenumber = lax.iota(jnp.int32, number)
    position = lax.iota(jnp.int32, length)
    phases = wavenumber[:, None] * position[None, :] % span_total
    angles = phases.astype(jnp.float32) * (2.0 * math.pi / span_total)
    return (jnp.cos(angles), jnp.sin(angles))


def weighting(number, span_total):
    wavenumber = lax.iota(jnp.int32, number)
    return (jnp.where(wavenumber == 0, 1.0, 2.0) / span_total).astype(jnp.float32)[:, None]


def forward_modes(cos_table, sin_table, field_rows):
    highest = lax.Precision.HIGHEST
    part_real = jnp.einsum("mz,pz->mp", cos_table, field_rows, precision=highest)
    part_imag = -jnp.einsum("mz,pz->mp", sin_table, field_rows, precision=highest)
    return jnp.concatenate([part_real, part_imag], axis=1)


def inverse_modes(cos_table, sin_table, mode_data, scaling, row_width):
    highest = lax.Precision.HIGHEST
    first = jnp.einsum(
        "mp,mz->pz", mode_data[:, :row_width] * scaling, cos_table, precision=highest
    )
    second = jnp.einsum(
        "mp,mz->pz", mode_data[:, row_width:] * scaling, sin_table, precision=highest
    )
    return first - second


def mix_modes(spectrum, weights, row_count, channels):
    highest = lax.Precision.HIGHEST
    mode_count = spectrum.shape[0]
    parts = spectrum.reshape(mode_count, 2, row_count, channels)
    blocks = weights.reshape(mode_count, 2, channels, channels)
    spec_real = parts[:, 0]
    spec_imag = parts[:, 1]
    mixed_real = jnp.einsum(
        "mrc,mco->mro", spec_real, blocks[:, 0], precision=highest
    ) - jnp.einsum("mrc,mco->mro", spec_imag, blocks[:, 1], precision=highest)
    mixed_imag = jnp.einsum(
        "mrc,mco->mro", spec_real, blocks[:, 1], precision=highest
    ) + jnp.einsum("mrc,mco->mro", spec_imag, blocks[:, 0], precision=highest)
    return jnp.concatenate(
        [
            mixed_real.reshape(mode_count, row_count * channels),
            mixed_imag.reshape(mode_count, row_count * channels),
        ],
        axis=1,
    )


def shards(features, spectral_weight, local_weight, bias_vector):
    rows_dev, channels, span_cells = features.shape
    span_count = lax.axis_size("span")
    span_total = span_cells * span_count
    modes_dev = spectral_weight.shape[0]
    modes_all = modes_dev * span_count
    weights = lax.all_gather(spectral_weight, "slab", axis=1, tiled=True)
    whole_weights = lax.all_gather(weights, "span", axis=0, tiled=True)
    line_data = lax.all_to_all(features, "span", split_axis=0, concat_axis=2, tiled=True)
    line_count = line_data.shape[0]
    line_width = line_count * channels
    line_rows = line_data.reshape(line_width, span_total)
    cos_table, sin_table = tables(modes_all, span_total, span_total)
    spectrum = forward_modes(cos_table, sin_table, line_rows)
    mixed = mix_modes(spectrum, whole_weights, line_count, channels)
    scaling = weighting(modes_all, span_total)
    returned = inverse_modes(cos_table, sin_table, mixed, scaling, line_width)
    returned = returned.reshape(line_count, channels, span_total)
    spectral = lax.all_to_all(returned, "span", split_axis=2, concat_axis=0, tiled=True)
    local_term = jnp.einsum("rcz,co->roz", features, local_weight, precision=lax.Precision.HIGHEST)
    return jax.nn.gelu(spectral + local_term + bias_vector[None, :, None], approximate=False)


def solution(mesh):
    placed = (P("slab", None, "span"), P("span", "slab"), P(), P())
    return jax.shard_map(
        shards, mesh=mesh, in_specs=placed, out_specs=P("slab", None, "span"), check_vma=False
    )
```

profile of v0, /device:TPU:0, one launch (start us, length us, event | category | flops | bytes accessed | tf_op | source)
XLA Modules:
  0.0 531.0 jit_solution(9405047965576421890)
XLA Ops:
  6.5 0.0 copy-start
  6.5 0.0 copy-start.2
  6.5 7.4 %all-to-all-start = ((f32[128,32,256]{2,1,0:T(8,128)}), f32[128,32,256]{2,1,0:T(8,128)}, u32[]{:S(2)}, u32[]{:S(2)}) async-start(f32[128,32,256]{2,1,0:T(8,128)} %param.4), calls=%async_computation | async-start | bytes 8388608 | tf_op jit(solution)/shard_map/all_to_all | solution.py:69
  14.0 0.0 all-gather.2.cloned.1.call-start
  14.0 0.0 copy-done.2
  14.0 7.6 %all_gather.6 = f32[64,2048]{1,0:T(8,128)} all-gather(f32[64,512]{1,0:T(8,128)S(1)} %copy-done.2), channel_id=1, replica_groups=mesh['span'=8,'slab'=4] {'slab'}, dimensions={1}, use_global_device_ids=true | all-gather | bytes 655360 | tf_op jit(solution)/shard_map/all_gather | solution.py:67
  21.7 0.0 all-gather.2.cloned.1.call-update
  21.7 136.3 %all-to-all-done = f32[128,32,256]{2,1,0:T(8,128)} async-done(((f32[128,32,256]{2,1,0:T(8,128)}), f32[128,32,256]{2,1,0:T(8,128)}, u32[]{:S(2)}, u32[]{:S(2)}) %all-to-all-start) | async-done | bytes 4194336 | tf_op jit(solution)/shard_map/all_to_all | solution.py:69
  158.0 5.5 %copy.19 = f32[8,16,32,256]{3,0,2,1:T(8,128)S(1)} copy(f32[8,16,32,256]{3,2,1,0:T(8,128)} %bitcast) | data formatting | bytes 8388608 | tf_op jit(solution)/shard_map/all_to_all | solution.py:69
  163.5 2.0 copy.36
  165.5 22.5 %fusion.42 = f32[512,512]{0,1:T(8,128)S(1)} fusion(f32[512,2048]{1,0:T(8,128)S(1)} %bitcast.71), kind=kOutput, calls=%fused_computation.48 | convolution fusion | flops 6457131008 | bytes 5242880 | tf_op jit(solution)/shard_map/mz,pz->mp/dot_general | solution.py:23
  188.0 23.2 %fusion.47 = f32[512,512]{0,1:T(8,128)} fusion(f32[512,2048]{1,0:T(8,128)S(1)} %bitcast.72), kind=kOutput, calls=%fused_computation.50 | convolution fusion | flops 6457393152 | bytes 5242880 | tf_op jit(solution)/shard_map/mz,pz->mp/dot_general | solution.py:24
  211.1 0.0 all-gather.2.cloned.1.call-done
  211.1 5.5 %copy.21 = f32[512,2048]{0,1:T(8,128)} copy(f32[512,2048]{1,0:T(8,128)} %all-gather.2.cloned.1.call-done) | data formatting | bytes 8388608 | tf_op jit(solution)/shard_map/all_gather | solution.py:68
  216.6 4.2 fusion.67
  220.8 8.4 %copy.35 = f32[512,1,32,32]{3,2,0,1:T(8,128)} copy(f32[512,1,32,32]{0,3,2,1:T(8,128)} %get-tuple-element.6) | data formatting | bytes 4194304
  229.2 1.4 pad_maximum_fusion
  230.6 1.2 fusion.68
  231.9 4.6 copy.32
  236.5 7.6 %copy.33 = f32[512,1,32,32]{3,2,0,1:T(8,128)} copy(f32[512,1,32,32]{0,3,2,1:T(8,128)S(1)} %get-tuple-element.5) | data formatting | bytes 4194304
  244.1 3.7 copy.34
  247.7 0.0 copy-start.1
  247.7 0.0 slice-start
  247.7 10.2 %fusion = f32[512,16,32]{2,1,0:T(8,128)S(1)} fusion(f32[512,1,32,32]{3,2,0,1:T(8,128)} %copy.35, f32[512,1,16,32]{3,2,0,1:T(8,128)} %copy.32), kind=kOutput, calls=%fused_computation | convolution fusion | flops 100663296 | bytes 4194304 | tf_op jit(solution)/shard_map/mrc,mco->mro/dot_general | solution.py:49
  257.9 0.0 copy-done.1
  258.0 0.0 slice-start.1
  258.0 10.8 %fusion.2 = f32[512,16,32]{2,1,0:T(8,128)} fusion(f32[512,1,32,32]{3,2,0,1:T(8,128)} %copy.35, f32[512,1,16,32]{3,2,0,1:T(8,128)S(1)} %copy-done.1), kind=kOutput, calls=%fused_computation.2 | convolution fusion | flops 100663296 | bytes 4194304 | tf_op jit(solution)/shard_map/mrc,mco->mro/dot_general | solution.py:48
  268.8 0.0 slice-done
  268.8 0.0 slice-done.1
  268.8 9.3 %fusion.33 = f32[512,16,32]{2,1,0:T(8,128)} fusion(f32[512,16,32]{2,1,0:T(8,128)S(1)} %fusion, f32[512,1,32,32]{3,2,0,1:T(8,128)S(1)} %bitcast.64, f32[512,1,16,32]{3,2,0,1:T(8,128)S(1)} %copy-done.1), kind=kOutput, calls=%fused_computation.43 | convolution fusion | flops 100925440 | bytes 5242880 | tf_op jit(solution)/shard_map/mrc,mco->mro/dot_general | solution.py:51
  278.1 2.8 copy.26
  280.9 12.4 %fusion.28 = f32[512,16,32]{2,1,0:T(8,128)} fusion(f32[512,16,32]{2,1,0:T(8,128)} %fusion.2, f32[512,1,32,32]{3,2,0,1:T(8,128)} %copy.33, f32[512,1,16,32]{3,2,0,1:T(8,128)} %copy.32), kind=kOutput, calls=%fused_computation.42 | convolution fusion | flops 100925440 | bytes 5242880 | tf_op jit(solution)/shard_map/mrc,mco->mro/dot_general | solution.py:46
  293.3 2.8 copy.25
  296.1 0.3 bitcast_multiply_fusion
  296.4 23.5 %fusion.40 = f32[512,2048]{1,0:T(8,128)S(1)} fusion(f32[512,512]{0,1:T(8,128)S(1)} %get-tuple-element.10), kind=kOutput, calls=%fused_computation.47 | convolution fusion | flops 6457131008 | bytes 5242880 | tf_op jit(solution)/shard_map/mp,mz->pz/dot_general | solution.py:30
  319.9 24.2 %convolution_subtract_fusion = f32[512,2048]{1,0:T(8,128)} fusion(f32[512,2048]{1,0:T(8,128)S(1)} %fusion.40, f32[512,512]{0,1:T(8,128)S(1)} %get-tuple-element.9), kind=kOutput, calls=%fused_computation.41 | convolution fusion | flops 6458179584 | bytes 9437184 | tf_op jit(solution)/shard_map/mp,mz->pz/dot_general | solution.py:33
  344.1 12.5 %copy.27 = f32[16,32,2048]{1,0,2:T(8,128)} copy(f32[16,32,2048]{2,1,0:T(8,128)} %bitcast.70) | data formatting | bytes 8388608 | tf_op jit(solution)/shard_map/reshape | solution.py:78
  356.6 12.8 %reshape.33 = f32[8,1,131072]{2,1,0:T(1,128)} reshape(f32[2048,16,32]{2,1,0:T(8,128)} %bitcast.65) | data formatting | bytes 8388608
  369.4 97.7 %all_to_all.33 = f32[8,1,131072]{2,1,0:T(1,128)} all-to-all(f32[8,1,131072]{2,1,0:T(1,128)} %reshape.33), channel_id=1, replica_groups=mesh['span'=8,'slab'=4] {'span'}, dimensions={0} | all-to-all | bytes 8388608 | tf_op jit(solution)/shard_map/all_to_all | solution.py:79
  467.2 0.6 broadcast.41
  467.7 13.8 %reduce = f32[8,131072]{1,0:T(8,128)} reduce(f32[8,1,131072]{2,1,0:T(1,128)} %all_to_all.33, f32[]{:T(128)} %broadcast.41), dimensions={1}, to_apply=%all_to_all.27.reduce_sub_computation | reduce | bytes 8388612 | tf_op jit(solution)/shard_map/all_to_all | solution.py:79
  481.5 13.4 %reshape.34 = f32[2048,16,32]{2,1,0:T(8,128)} reshape(f32[8,131072]{1,0:T(8,128)} %reduce) | data formatting | bytes 8388608
  494.9 0.0 copy-start.3
  494.9 13.1 %copy.28 = f32[16,32,8,256]{3,1,0,2:T(8,128)} copy(f32[16,32,8,256]{1,0,3,2:T(8,128)} %bitcast.66) | data formatting | bytes 8388608 | tf_op jit(solution)/shard_map/all_to_all | solution.py:79
  507.9 0.0 copy-done
  507.9 0.0 copy-done.3
  507.9 16.0 %fusion.12 = f32[128,32,256]{2,1,0:T(8,128)} fusion(f32[16,32,8,256]{3,1,0,2:T(8,128)} %copy.28, f32[128,32,256]{2,1,0:T(8,128)} %param.4, f32[32]{0:T(128)S(1)} %copy-done.3, f32[32,32]{1,0:T(8,128)S(1)} %copy-done), kind=kOutput, calls=%fused_computation.16 | convolution fusion | flops 471859200 | bytes 12587136 | tf_op jit(solution)/shard_map/rcz,co->roz/dot_general | solution.py:80
  (2 shorter events, 0.0 us)
Async XLA Ops:
  6.5 501.4 %copy-start = (f32[32,32]{1,0:T(8,128)S(1)}, f32[32,32]{1,0:T(8,128)}, u32[]{:S(2)}) copy-start(f32[32,32]{1,0:T(8,128)} %param.6) | copy-start | bytes 12292
  6.5 7.5 %copy-start.2 = (f32[64,512]{1,0:T(8,128)S(1)}, f32[64,512]{1,0:T(8,128)}, u32[]{:S(2)}) copy-start(f32[64,512]{1,0:T(8,128)} %param.5) | copy-start | bytes 393220
  6.5 151.4 %all-to-all-start = ((f32[128,32,256]{2,1,0:T(8,128)}), f32[128,32,256]{2,1,0:T(8,128)}, u32[]{:S(2)}, u32[]{:S(2)}) async-start(f32[128,32,256]{2,1,0:T(8,128)} %param.4), calls=%async_computation | async-start | bytes 8388608 | tf_op jit(solution)/shard_map/all_to_all | solution.py:69
  14.0 197.2 %all-gather.2.cloned.1.call-start = ((), (), s32[]{:S(2)}) async-start(), calls=%async_computation.2 | async-start | bytes 4718592 | tf_op jit(solution)/shard_map/all_gather | solution.py:68
  247.7 10.2 %copy-start.1 = (f32[512,1,16,32]{3,2,0,1:T(8,128)S(1)}, f32[512,1,16,32]{3,2,0,1:T(8,128)}, u32[]{:S(2)}) copy-start(f32[512,1,16,32]{3,2,0,1:T(8,128)} %copy.34) | copy-start | bytes 3145732
  247.7 21.1 %slice-start = ((s8[8388608]{0:T(1024)(128)(4,1)}), s8[4194304]{0:T(1024)(128)(4,1)S(1)}, s32[]{:S(2)}) async-start(s8[8388608]{0:T(1024)(128)(4,1)} %bitcast.63), calls=%async_computation.3 | async-start | bytes 8388608
  258.0 10.9 %slice-start.1 = ((s8[8388608]{0:T(1024)(128)(4,1)}), s8[4194304]{0:T(1024)(128)(4,1)S(1)}, s32[]{:S(2)}) async-start(s8[8388608]{0:T(1024)(128)(4,1)} %bitcast.63), calls=%async_computation.4 | async-start | bytes 8388608
  494.9 13.1 %copy-start.3 = (f32[32]{0:T(128)S(1)}, f32[32]{0:T(128)}, u32[]{:S(2)}) copy-start(f32[32]{0:T(128)} %param.7) | copy-start | bytes 388
Sparse Core Ops, SparseCore 0:
  21.8 131.8 all-gather.1
where the time goes:
time: 537 us; the launch traced here: 531 us
  matrix products  152 us (28%)
  waiting for transfers between devices  136 us (25%)
  blocking collectives  105 us (20%)
  local copies, waits for them, and re-layouts  101 us (19%)
  other arithmetic  15.4 us (3%)
  between operations  13.7 us (3%)
  starting transfers between devices  7.45 us (1%)
    all_to_all x1, waiting for transfers between devices, shards(): lax.all_to_all(features, 'span', split_axis=0, concat_axis=2, tiled=True)  136 us
    all_to_all x1, blocking collectives, shards(): lax.all_to_all(returned, 'span', split_axis=2, concat_axis=0, tiled=True)  97.7 us
    unnamed x19, local copies, waits for them, and re-layouts  52.4 us
    dot_general x1, matrix products, inverse_modes(): jnp.einsum('mp,mz->pz', mode_data[:, row_width:] * scaling, sin_table, pr...  24.2 us
    dot_general x1, matrix products, inverse_modes(): jnp.einsum('mp,mz->pz', mode_data[:, :row_width] * scaling, cos_table, pr...  23.5 us
    dot_general x1, matrix products, forward_modes(): jnp.einsum('mz,pz->mp', sin_table, field_rows, precision=highest)  23.2 us
    dot_general x1, matrix products, forward_modes(): jnp.einsum('mz,pz->mp', cos_table, field_rows, precision=highest)  22.5 us
    dot_general x1, matrix products, shards(): jnp.einsum('rcz,co->roz', features, local_weight, precision=lax.Precision...  16 us
  transfers between devices with their start and end apart: 2, of which 1 were waited for; matrix products, arithmetic and copies ran while one was open for 10% of the time, Pallas kernels for 0%

commit v1 on v0

--- a/solution.py
+++ b/solution.py
@@ -3,6 +3,28 @@
 import jax.numpy as jnp
 from jax import lax
 from jax.sharding import PartitionSpec as P
+
+
+def split_up(value, dim, length):
+    before, after = (value.shape[:dim], value.shape[dim + 1 :])
+    return jnp.moveaxis(value.reshape(*before, length, -1, *after), dim, 0)
+
+
+def in_order(blocks, dim):
+    dims = list(blocks.shape[1:])
+    dims[dim] *= blocks.shape[0]
+    return jnp.moveaxis(blocks, 0, dim).reshape(dims)
+
+
+def sent_to_each(x, axis, split_dim, concat_dim):
+    count, here = (lax.axis_size(axis), lax.axis_index(axis))
+    blocks = split_up(x, split_dim, count)
+    finished = [blocks[here]]
+    for turn in range(1, count):
+        sent = blocks[(here + turn) % count]
+        finished.append(lax.ppermute(sent, axis, [(i, (i + turn) % count) for i in range(count)]))
+    blocks = jnp.stack(finished)[(here - jnp.arange(count)) % count]
+    return in_order(blocks, concat_dim)
 
 
 def tables(number, length, span_total):
@@ -66,7 +88,7 @@
     modes_all = modes_dev * span_count
     weights = lax.all_gather(spectral_weight, "slab", axis=1, tiled=True)
     whole_weights = lax.all_gather(weights, "span", axis=0, tiled=True)
-    line_data = lax.all_to_all(features, "span", split_axis=0, concat_axis=2, tiled=True)
+    line_data = sent_to_each(features, "span", 0, 2)
     line_count = line_data.shape[0]
     line_width = line_count * channels
     line_rows = line_data.reshape(line_width, span_total)

time: 537 us -> 549 us (1.022)
  waiting for transfers between devices: 136 us -> 61.2 us
  blocking collectives: 105 us -> 159 us
  starting transfers between devices: 7.45 us -> 30.5 us
  local copies, waits for them, and re-layouts: 101 us -> 113 us
    all_to_all x1 -> x0, waiting for transfers between devices: 136 us -> none  [shards(): lax.all_to_all(features, 'span', split_axis=0, concat_axis=2, tiled=True)]
    ppermute x0 -> x7, waiting for transfers between devices: none -> 61.2 us  [sent_to_each(): lax.ppermute(sent, axis, [(i, (i + turn) % count) for i in range(count)])]
    all_to_all x1, blocking collectives: 97.7 us -> 149 us  [shards(): lax.all_to_all(returned, 'span', split_axis=2, concat_axis=0, tiled=True)]
    ppermute x0 -> x7, starting transfers between devices: none -> 30.5 us  [sent_to_each(): lax.ppermute(sent, axis, [(i, (i + turn) % count) for i in range(count)])]
    all_to_all x1 -> x0, starting transfers between devices: 7.41 us -> none  [shards(): lax.all_to_all(features, 'span', split_axis=0, concat_axis=2, tiled=True)]
    all_to_all x1 -> x0, local copies, waits for them, and re-layouts: 5.49 us -> none  [shards(): lax.all_to_all(features, 'span', split_axis=0, concat_axis=2, tiled=True)]
    transpose x0 -> x1, local copies, waits for them, and re-layouts: none -> 5.49 us  [in_order(): return jnp.moveaxis(blocks, 0, dim).reshape(dims)]
    unnamed x19 -> x25, local copies, waits for them, and re-layouts: 52.4 us -> 56.7 us
  transfers between devices with their start and end apart: 2 -> 8, of which waited for: 1 -> 3; matrix products, arithmetic and copies ran while one was open for 10% -> 14% of each run, Pallas kernels for 0% -> 0%
where the time goes in v1:
time: 549 us; the launch traced here: 542 us
  blocking collectives  159 us (29%)
  matrix products  150 us (27%)
  local copies, waits for them, and re-layouts  113 us (21%)
  waiting for transfers between devices  61.2 us (11%)
  starting transfers between devices  30.5 us (6%)
  other arithmetic  14.2 us (3%)
  between operations  13.9 us (3%)
    all_to_all x1, blocking collectives, shards(): lax.all_to_all(returned, 'span', split_axis=2, concat_axis=0, tiled=True)  149 us
    ppermute x7, waiting for transfers between devices, sent_to_each(): lax.ppermute(sent, axis, [(i, (i + turn) % count) for i in range(count)])  61.2 us
    unnamed x25, local copies, waits for them, and re-layouts  56.7 us
    ppermute x7, starting transfers between devices, sent_to_each(): lax.ppermute(sent, axis, [(i, (i + turn) % count) for i in range(count)])  30.5 us
    dot_general x1, matrix products, inverse_modes(): jnp.einsum('mp,mz->pz', mode_data[:, row_width:] * scaling, sin_table, pr...  24.2 us
    dot_general x1, matrix products, inverse_modes(): jnp.einsum('mp,mz->pz', mode_data[:, :row_width] * scaling, cos_table, pr...  23.4 us
    dot_general x1, matrix products, forward_modes(): jnp.einsum('mz,pz->mp', cos_table, field_rows, precision=highest)  22.7 us
    dot_general x1, matrix products, forward_modes(): jnp.einsum('mz,pz->mp', sin_table, field_rows, precision=highest)  22.3 us
  transfers between devices with their start and end apart: 8, of which 3 were waited for; matrix products, arithmetic and copies ran while one was open for 14% of the time, Pallas kernels for 0%

profile of v1, /device:TPU:0, one launch (start us, length us, event | category | flops | bytes accessed | tf_op | source)
XLA Modules:
  0.0 541.9 jit_solution(16425208556676676037)
XLA Ops:
  6.5 0.0 copy-start
  6.5 0.0 all-gather.2.cloned.1.call-start
  6.5 10.4 %all_gather.6 = f32[64,2048]{1,0:T(8,128)} all-gather(f32[64,512]{1,0:T(8,128)} %param.5), channel_id=1, replica_groups=mesh['span'=8,'slab'=4] {'slab'}, dimensions={1}, use_global_device_ids=true | all-gather | bytes 655360 | tf_op jit(solution)/shard_map/all_gather | solution.py:89
  16.9 0.0 all-gather.2.cloned.1.call-update
  17.0 3.4 dynamic-slice_bitcast_fusion
  20.4 1.5 collective-permute-start
  21.9 1.6 collective-permute-start.1
  23.4 2.6 collective-permute-start.2
  26.0 1.2 collective-permute-start.3
  27.2 2.6 collective-permute-start.4
  29.9 14.8 %collective-permute-done = f32[16,32,256]{2,1,0:T(8,128)S(1)} collective-permute-done((f32[16,32,256]{2,1,0:T(8,128)S(1)}, f32[16,32,256]{2,1,0:T(8,128)S(1)}, u32[]{:S(2)}, u32[]{:S(2)}) %collective-permute-start) | collective-permute-done | bytes 524320 | tf_op jit(solution)/shard_map/ppermute | solution.py:25
  44.6 8.5 %collective-permute-start.5 = (f32[16,32,256]{2,1,0:T(8,128)S(1)}, f32[16,32,256]{2,1,0:T(8,128)S(1)}, u32[]{:S(2)}, u32[]{:S(2)}) collective-permute-start(f32[16,32,256]{2,1,0:T(8,128)S(1)} %get-tuple-element.8), channel_id=1, source_target_pairs={{0,24},{4,28},{8,0},{12,4},{16,8},{20,12},{24,16},{28,20},{1,25},{... | collective-permute-start | bytes 1572872 | tf_op jit(solution)/shard_map/ppermute | solution.py:25
  53.2 0.8 bitcast_dynamic-update-slice_fusion.6
  54.0 0.0 collective-permute-done.1
  54.0 12.5 %collective-permute-start.6 = (f32[16,32,256]{2,1,0:T(8,128)S(1)}, f32[16,32,256]{2,1,0:T(8,128)S(1)}, u32[]{:S(2)}, u32[]{:S(2)}) collective-permute-start(f32[16,32,256]{2,1,0:T(8,128)S(1)} %get-tuple-element.7), channel_id=1, source_target_pairs={{0,28},{4,0},{8,4},{12,8},{16,12},{20,16},{24,20},{28,24},{1,29},{... | collective-permute-start | bytes 1572872 | tf_op jit(solution)/shard_map/ppermute | solution.py:25
  66.5 0.8 bitcast_dynamic-update-slice_fusion.5
  67.3 31.9 %collective-permute-done.2 = f32[16,32,256]{2,1,0:T(8,128)S(1)} collective-permute-done((f32[16,32,256]{2,1,0:T(8,128)S(1)}, f32[16,32,256]{2,1,0:T(8,128)S(1)}, u32[]{:S(2)}, u32[]{:S(2)}) %collective-permute-start.2) | collective-permute-done | bytes 524320 | tf_op jit(solution)/shard_map/ppermute | solution.py:25
  99.3 0.8 bitcast_dynamic-update-slice_fusion.4
  100.1 0.0 collective-permute-done.3
  100.1 0.8 bitcast_dynamic-update-slice_fusion.3
  100.9 0.0 collective-permute-done.4
  100.9 0.8 bitcast_dynamic-update-slice_fusion.2
  101.8 0.0 collective-permute-done.5
  101.8 0.8 bitcast_dynamic-update-slice_fusion.1
  102.6 14.5 %collective-permute-done.6 = f32[16,32,256]{2,1,0:T(8,128)S(1)} collective-permute-done((f32[16,32,256]{2,1,0:T(8,128)S(1)}, f32[16,32,256]{2,1,0:T(8,128)S(1)}, u32[]{:S(2)}, u32[]{:S(2)}) %collective-permute-start.6) | collective-permute-done | bytes 524320 | tf_op jit(solution)/shard_map/ppermute | solution.py:25
  117.1 0.8 bitcast_dynamic-update-slice_fusion
  117.9 5.0 gather_fusion
  122.9 5.5 %copy.28 = f32[16,32,8,256]{3,2,1,0:T(8,128)S(1)} copy(f32[16,32,8,256]{3,1,0,2:T(8,128)} %bitcast.98) | data formatting | bytes 8388608 | tf_op jit(solution)/shard_map/transpose | solution.py:16
  128.4 2.0 copy.45
  130.4 22.7 %fusion.42 = f32[512,512]{0,1:T(8,128)S(1)} fusion(f32[512,2048]{1,0:T(8,128)S(1)} %bitcast.102), kind=kOutput, calls=%fused_computation.49 | convolution fusion | flops 6457131008 | bytes 5242880 | tf_op jit(solution)/shard_map/mz,pz->mp/dot_general | solution.py:45
  153.1 22.3 %fusion.47 = f32[512,512]{0,1:T(8,128)S(1)} fusion(f32[512,2048]{1,0:T(8,128)S(1)} %bitcast.103), kind=kOutput, calls=%fused_computation.51 | convolution fusion | flops 6457393152 | bytes 5242880 | tf_op jit(solution)/shard_map/mz,pz->mp/dot_general | solution.py:46
  175.4 0.2 pad_maximum_fusion
  175.6 0.2 fusion.70
  175.8 3.9 copy.41
  179.7 3.7 copy.43
  183.4 0.0 all-gather.2.cloned.1.call-done
  183.4 5.3 copy.30
  188.7 4.2 fusion.69
  193.0 8.3 %copy.44 = f32[512,1,32,32]{3,2,0,1:T(8,128)} copy(f32[512,1,32,32]{0,3,2,1:T(8,128)} %get-tuple-element.6) | data formatting | bytes 4194304
  201.3 7.6 %copy.42 = f32[512,1,32,32]{3,2,0,1:T(8,128)} copy(f32[512,1,32,32]{0,3,2,1:T(8,128)S(1)} %get-tuple-element.5) | data formatting | bytes 4194304
  208.9 10.5 %fusion = f32[512,16,32]{2,1,0:T(8,128)S(1)} fusion(f32[512,1,32,32]{3,2,0,1:T(8,128)} %copy.44, f32[512,1,16,32]{3,2,0,1:T(8,128)} %copy.41), kind=kOutput, calls=%fused_computation.1 | convolution fusion | flops 100663296 | bytes 4194304 | tf_op jit(solution)/shard_map/mrc,mco->mro/dot_general | solution.py:71
  219.4 0.0 copy-done.1
  219.5 0.0 copy-done.2
  219.5 0.0 slice-start.1
  219.5 9.1 %fusion.2 = f32[512,16,32]{2,1,0:T(8,128)} fusion(f32[512,1,32,32]{3,2,0,1:T(8,128)S(1)} %copy-done.1, f32[512,1,16,32]{3,2,0,1:T(8,128)S(1)} %copy-done.2), kind=kOutput, calls=%fused_computation.3 | convolution fusion | flops 100663296 | bytes 4194304 | tf_op jit(solution)/shard_map/mrc,mco->mro/dot_general | solution.py:70
  228.6 0.0 slice-done
  228.6 0.0 slice-done.1
  228.6 9.5 %fusion.33 = f32[512,16,32]{2,1,0:T(8,128)} fusion(f32[512,16,32]{2,1,0:T(8,128)S(1)} %fusion, f32[512,1,32,32]{3,2,0,1:T(8,128)S(1)} %bitcast.94, f32[512,1,16,32]{3,2,0,1:T(8,128)S(1)} %copy-done.2), kind=kOutput, calls=%fused_computation.44 | convolution fusion | flops 100925440 | bytes 5242880 | tf_op jit(solution)/shard_map/mrc,mco->mro/dot_general | solution.py:73
  238.1 2.8 copy.35
  240.9 12.4 %fusion.28 = f32[512,16,32]{2,1,0:T(8,128)} fusion(f32[512,16,32]{2,1,0:T(8,128)} %fusion.2, f32[512,1,32,32]{3,2,0,1:T(8,128)} %copy.42, f32[512,1,16,32]{3,2,0,1:T(8,128)} %copy.41), kind=kOutput, calls=%fused_computation.43 | convolution fusion | flops 100925440 | bytes 5242880 | tf_op jit(solution)/shard_map/mrc,mco->mro/dot_general | solution.py:68
  253.3 2.8 copy.34
  256.1 0.3 bitcast_multiply_fusion
  256.3 23.4 %fusion.40 = f32[512,2048]{1,0:T(8,128)S(1)} fusion(f32[512,512]{0,1:T(8,128)S(1)} %get-tuple-element.18), kind=kOutput, calls=%fused_computation.48 | convolution fusion | flops 6457131008 | bytes 5242880 | tf_op jit(solution)/shard_map/mp,mz->pz/dot_general | solution.py:52
  279.8 24.2 %convolution_subtract_fusion = f32[512,2048]{1,0:T(8,128)} fusion(f32[512,2048]{1,0:T(8,128)S(1)} %fusion.40, f32[512,512]{0,1:T(8,128)S(1)} %get-tuple-element.17), kind=kOutput, calls=%fused_computation.42 | convolution fusion | flops 6458179584 | bytes 9437184 | tf_op jit(solution)/shard_map/mp,mz->pz/dot_general | solution.py:55
  304.0 12.5 %copy.36 = f32[16,32,2048]{1,0,2:T(8,128)} copy(f32[16,32,2048]{2,1,0:T(8,128)} %bitcast.101) | data formatting | bytes 8388608 | tf_op jit(solution)/shard_map/reshape | solution.py:100
  316.5 12.8 %reshape.89 = f32[8,1,131072]{2,1,0:T(1,128)} reshape(f32[2048,16,32]{2,1,0:T(8,128)} %bitcast.95) | data formatting | bytes 8388608
  329.3 148.7 %all_to_all.18 = f32[8,1,131072]{2,1,0:T(1,128)} all-to-all(f32[8,1,131072]{2,1,0:T(1,128)} %reshape.89), channel_id=1, replica_groups=mesh['span'=8,'slab'=4] {'span'}, dimensions={0} | all-to-all | bytes 8388608 | tf_op jit(solution)/shard_map/all_to_all | solution.py:101
  478.0 0.5 broadcast.117
  478.5 13.7 %reduce = f32[8,131072]{1,0:T(8,128)} reduce(f32[8,1,131072]{2,1,0:T(1,128)} %all_to_all.18, f32[]{:T(128)} %broadcast.117), dimensions={1}, to_apply=%all_to_all.13.reduce_sub_computation | reduce | bytes 8388612 | tf_op jit(solution)/shard_map/all_to_all | solution.py:101
  492.3 13.4 %reshape.90 = f32[2048,16,32]{2,1,0:T(8,128)} reshape(f32[8,131072]{1,0:T(8,128)} %reduce) | data formatting | bytes 8388608
  505.6 13.1 %copy.37 = f32[16,32,8,256]{3,1,0,2:T(8,128)} copy(f32[16,32,8,256]{1,0,3,2:T(8,128)} %bitcast.96) | data formatting | bytes 8388608 | tf_op jit(solution)/shard_map/all_to_all | solution.py:101
  518.7 0.0 copy-done
  518.7 0.0 copy-done.3
  518.7 16.1 %fusion.12 = f32[128,32,256]{2,1,0:T(8,128)} fusion(f32[16,32,8,256]{3,1,0,2:T(8,128)} %copy.37, f32[128,32,256]{2,1,0:T(8,128)} %param.4, f32[32]{0:T(128)S(1)} %copy-done.3, f32[32,32]{1,0:T(8,128)S(1)} %copy-done), kind=kOutput, calls=%fused_computation.17 | convolution fusion | flops 471859200 | bytes 12587136 | tf_op jit(solution)/shard_map/rcz,co->roz/dot_general | solution.py:102
  (8 shorter events, 0.0 us)
Async XLA Ops:
  6.5 512.2 %copy-start = (f32[32,32]{1,0:T(8,128)S(1)}, f32[32,32]{1,0:T(8,128)}, u32[]{:S(2)}) copy-start(f32[32,32]{1,0:T(8,128)} %param.6) | copy-start | bytes 12292
  6.5 176.9 %all-gather.2.cloned.1.call-start = ((), (), s32[]{:S(2)}) async-start(), calls=%async_computation.1 | async-start | bytes 4718592 | tf_op jit(solution)/shard_map/all_gather | solution.py:90
  20.4 24.3 %collective-permute-start = (f32[16,32,256]{2,1,0:T(8,128)S(1)}, f32[16,32,256]{2,1,0:T(8,128)S(1)}, u32[]{:S(2)}, u32[]{:S(2)}) collective-permute-start(f32[16,32,256]{2,1,0:T(8,128)S(1)} %get-tuple-element.13), channel_id=1, source_target_pairs={{0,4},{4,8},{8,12},{12,16},{16,20},{20,24},{24,28},{28,0},{1,5},{5... | collective-permute-start | bytes 1572872 | tf_op jit(solution)/shard_map/ppermute | solution.py:25
  21.9 32.2 %collective-permute-start.1 = (f32[16,32,256]{2,1,0:T(8,128)S(1)}, f32[16,32,256]{2,1,0:T(8,128)S(1)}, u32[]{:S(2)}, u32[]{:S(2)}) collective-permute-start(f32[16,32,256]{2,1,0:T(8,128)S(1)} %get-tuple-element.12), channel_id=1, source_target_pairs={{0,8},{4,12},{8,16},{12,20},{16,24},{20,28},{24,0},{28,4},{1,9},{5... | collective-permute-start | bytes 1572872 | tf_op jit(solution)/shard_map/ppermute | solution.py:25
  23.4 75.8 %collective-permute-start.2 = (f32[16,32,256]{2,1,0:T(8,128)S(1)}, f32[16,32,256]{2,1,0:T(8,128)S(1)}, u32[]{:S(2)}, u32[]{:S(2)}) collective-permute-start(f32[16,32,256]{2,1,0:T(8,128)S(1)} %get-tuple-element.11), channel_id=1, source_target_pairs={{0,12},{4,16},{8,20},{12,24},{16,28},{20,0},{24,4},{28,8},{1,13},{... | collective-permute-start | bytes 1572872 | tf_op jit(solution)/shard_map/ppermute | solution.py:25
  26.0 74.1 %collective-permute-start.3 = (f32[16,32,256]{2,1,0:T(8,128)S(1)}, f32[16,32,256]{2,1,0:T(8,128)S(1)}, u32[]{:S(2)}, u32[]{:S(2)}) collective-permute-start(f32[16,32,256]{2,1,0:T(8,128)S(1)} %get-tuple-element.10), channel_id=1, source_target_pairs={{0,16},{4,20},{8,24},{12,28},{16,0},{20,4},{24,8},{28,12},{1,17},{... | collective-permute-start | bytes 1572872 | tf_op jit(solution)/shard_map/ppermute | solution.py:25
  27.2 73.7 %collective-permute-start.4 = (f32[16,32,256]{2,1,0:T(8,128)S(1)}, f32[16,32,256]{2,1,0:T(8,128)S(1)}, u32[]{:S(2)}, u32[]{:S(2)}) collective-permute-start(f32[16,32,256]{2,1,0:T(8,128)S(1)} %get-tuple-element.9), channel_id=1, source_target_pairs={{0,20},{4,24},{8,28},{12,0},{16,4},{20,8},{24,12},{28,16},{1,21},{... | collective-permute-start | bytes 1572872 | tf_op jit(solution)/shard_map/ppermute | solution.py:25
  44.6 57.1 %collective-permute-start.5 = (f32[16,32,256]{2,1,0:T(8,128)S(1)}, f32[16,32,256]{2,1,0:T(8,128)S(1)}, u32[]{:S(2)}, u32[]{:S(2)}) collective-permute-start(f32[16,32,256]{2,1,0:T(8,128)S(1)} %get-tuple-element.8), channel_id=1, source_target_pairs={{0,24},{4,28},{8,0},{12,4},{16,8},{20,12},{24,16},{28,20},{1,25},{... | collective-permute-start | bytes 1572872 | tf_op jit(solution)/shard_map/ppermute | solution.py:25
  54.0 63.1 %collective-permute-start.6 = (f32[16,32,256]{2,1,0:T(8,128)S(1)}, f32[16,32,256]{2,1,0:T(8,128)S(1)}, u32[]{:S(2)}, u32[]{:S(2)}) collective-permute-start(f32[16,32,256]{2,1,0:T(8,128)S(1)} %get-tuple-element.7), channel_id=1, source_target_pairs={{0,28},{4,0},{8,4},{12,8},{16,12},{20,16},{24,20},{28,24},{1,29},{... | collective-permute-start | bytes 1572872 | tf_op jit(solution)/shard_map/ppermute | solution.py:25
  208.9 10.5 %copy-start.1 = (f32[512,1,32,32]{3,2,0,1:T(8,128)S(1)}, f32[512,1,32,32]{3,2,0,1:T(8,128)}, u32[]{:S(2)}) copy-start(f32[512,1,32,32]{3,2,0,1:T(8,128)} %copy.44) | copy-start | bytes 6291460
  208.9 10.5 %copy-start.2 = (f32[512,1,16,32]{3,2,0,1:T(8,128)S(1)}, f32[512,1,16,32]{3,2,0,1:T(8,128)}, u32[]{:S(2)}) copy-start(f32[512,1,16,32]{3,2,0,1:T(8,128)} %copy.43) | copy-start | bytes 3145732
  208.9 19.7 %slice-start = ((s8[8388608]{0:T(1024)(128)(4,1)}), s8[4194304]{0:T(1024)(128)(4,1)S(1)}, s32[]{:S(2)}) async-start(s8[8388608]{0:T(1024)(128)(4,1)} %bitcast.93), calls=%async_computation.2 | async-start | bytes 8388608
  219.5 9.1 %slice-start.1 = ((s8[8388608]{0:T(1024)(128)(4,1)}), s8[4194304]{0:T(1024)(128)(4,1)S(1)}, s32[]{:S(2)}) async-start(s8[8388608]{0:T(1024)(128)(4,1)} %bitcast.93), calls=%async_computation.3 | async-start | bytes 8388608
  505.6 13.1 %copy-start.3 = (f32[32]{0:T(128)S(1)}, f32[32]{0:T(128)}, u32[]{:S(2)}) copy-start(f32[32]{0:T(128)} %param.7) | copy-start | bytes 388
Sparse Core Ops, SparseCore 0:
  17.0 136.8 all-gather.1
